TPU v7x, 256 devices: a whole 4x4x8 slice. The times are simulated.
256 devices in a mesh: slab: 64 (over y, x_hi, z), sub: 4 (over x_lo, core).
Axes of the slice: x: 4 (x_hi: 2, x_lo: 2; x = x_hi * 2 + x_lo), y: 4, z: 8, core: 2. Of those that a mesh axis runs over, the one named last changes fastest.
Arguments:
- right_sides: bfloat16 [524288, 768], P(('slab', 'sub')), may hold values from -6 to 6
- front_sides: bfloat16 [131072, 768], P(('slab', 'sub')), may hold values from -6 to 6
- pending_front: bfloat16 [131072, 256], P(('slab', 'sub')), may hold values from -6 to 6
- inner_index: int32 [4096, 6], P(('slab', 'sub')), may hold values from 0 to 15, all different within a row
- inner_blocks: bfloat16 [4096, 6, 128, 128], P(('slab', 'sub')), may hold values from -0.15625 to 0.15625
- inner_inverse: bfloat16 [4096, 128, 128], P(('slab', 'sub')), may hold values from -1 to 2
- outer_index: int32 [1024, 8], P(('slab', 'sub')), may hold values from 0 to 15, all different within a row
- outer_blocks: bfloat16 [1024, 8, 128, 128], P(('slab', 'sub')), may hold values from -0.125 to 0.125
- front_inverse: bfloat16 [1024, 128, 128], P(('slab', 'sub')), may hold values from -1 to 2
Outputs:
- solution: bfloat16 [524288, 768], P(('slab', 'sub'))
- front_solution: bfloat16 [131072, 768], P(('slab', 'sub'))
All inputs are finite; a program needn't handle non-finite values.
Results may differ from a plain program's by a relative error of at most 0.009.
Values may be sent and summed in bfloat16 or wider, within the bound.
A program may use at most 64 MiB of HBM per device.

v0:
```python
import jax
import jax.numpy as jnp
from jax import lax
from jax.sharding import PartitionSpec as P


def passed_along(x, axis, by):
    size = lax.axis_size(axis)
    pairs = [(i, i + by) for i in range(size) if 0 <= i + by < size]
    return lax.ppermute(x, axis, pairs)


def collect(share):
    return lax.all_gather(share, "sub", axis=0, tiled=True)


def shards(
    right_sides,
    front_sides,
    pending_front,
    inner_index,
    inner_blocks,
    inner_inverse,
    outer_index,
    outer_blocks,
    front_inverse,
):
    block_size = inner_inverse.shape[1]
    inner_rows = inner_inverse.shape[0]
    outer_rows = front_inverse.shape[0]
    columns = pending_front.shape[1]
    groups = right_sides.shape[1] // columns
    gathered = collect(pending_front)
    solved_list = []
    front_list = []
    for group in range(groups):
        front_blocks = gathered.reshape(-1, block_size, columns)
        picked = jnp.take(front_blocks, inner_index, axis=0)
        coupled = jnp.einsum(
            "ikab,ikbc->iac", inner_blocks, picked, preferred_element_type=jnp.float32
        )
        group_sides = right_sides[:, group * columns : (group + 1) * columns].reshape(
            inner_rows, block_size, columns
        )
        inner_values = (group_sides.astype(jnp.float32) - coupled).astype(jnp.bfloat16)
        solved = jnp.einsum(
            "iab,ibc->iac", inner_inverse, inner_values, preferred_element_type=jnp.float32
        ).astype(jnp.bfloat16)
        chosen = jnp.take(solved, outer_index, axis=0)
        outgoing = jnp.einsum(
            "jkab,jkbc->jac", outer_blocks, chosen, preferred_element_type=jnp.float32
        )
        outer_sides = front_sides[:, group * columns : (group + 1) * columns].reshape(
            outer_rows, block_size, columns
        )
        outer_values = (outer_sides.astype(jnp.float32) - outgoing).astype(jnp.bfloat16)
        front_done = jnp.einsum(
            "jab,jbc->jac", front_inverse, outer_values, preferred_element_type=jnp.float32
        ).astype(jnp.bfloat16)
        front_done = front_done.reshape(-1, columns)
        solved_list.append(solved.reshape(-1, columns))
        front_list.append(front_done)
        if group + 1 < groups:
            gathered = passed_along(collect(front_done), "slab", 1)
    solution = jnp.concatenate(solved_list, axis=1)
    front_solution = jnp.concatenate(front_list, axis=1)
    return (solution, front_solution)


def solution(mesh):
    placed = (
        P(("slab", "sub"), None),
        P(("slab", "sub"), None),
        P(("slab", "sub"), None),
        P(("slab", "sub"), None),
        P(("slab", "sub"), None, None, None),
        P(("slab", "sub"), None, None),
        P(("slab", "sub"), None),
        P(("slab", "sub"), None, None, None),
        P(("slab", "sub"), None, None),
    )
    return jax.shard_map(
        shards,
        mesh=mesh,
        in_specs=placed,
        out_specs=(P(("slab", "sub"), None), P(("slab", "sub"), None)),
        check_vma=False,
    )
```

profile of v0, /device:TPU:25, one launch (start us, length us, event | category | flops | bytes accessed | tf_op | source)
XLA Modules:
  0.0 216.4 jit_solution(2010275956903110285)
XLA Ops:
  8.0 0.8 compare_and_fusion
  11.3 2.0 fusion.115
  13.2 3.6 %fusion.114 = (bf16[2048,256]{1,0:T(8,128)(2,1)}, bf16[2048,256]{1,0:T(8,128)(2,1)}, bf16[2048,256]{1,0:T(8,128)(2,1)}) fusion(bf16[2048,768]{1,0:T(8,128)(2,1)} %param.13), kind=kLoop, calls=%fused_computation.74 | loop fusion | bytes 6291456 | tf_op jit(solution)/shard_map/slice | solution.py:42
  16.8 19.3 %all-gather.4.cloned.1.call-done = bf16[2048,256]{1,0:T(8,128)(2,1)} async-done(((bf16[512,256]{1,0:T(8,128)(2,1)}), bf16[2048,256]{1,0:T(8,128)(2,1)}) %all-gather.4.cloned.1.call-update) | async-done | bytes 1048592 | tf_op jit(solution)/shard_map/all_gather | solution.py:14
  36.1 7.2 %gather_fusion = bf16[96,128,256]{2,1,0:T(8,128)(2,1)} fusion(bf16[16,128,256]{2,1,0:T(8,128)(2,1)} %bitcast.123, s32[1024]{0:T(1024)S(1)} %pad_clamp_fusion.1), kind=kCustom, calls=%fused_computation.clone | custom fusion | bytes 12583296 | tf_op jit(solution)/shard_map/jit(_take)/gather | solution.py:38
  43.4 6.0 %fusion.45 = bf16[16,256,128]{1,2,0:T(8,128)(2,1)} fusion(bf16[16,128,128]{2,1,0:T(8,128)(2,1)} %param.18, bf16[16,128,256]{2,1,0:T(8,128)(2,1)} %bitcast.142, bf16[16,6,128,128]{3,2,1,0:T(8,128)(2,1)S(1)} %copy-done, bf16[16,6,128,256]{3,2,1,0:T(8,128)(2,1)} %bitcast.131, pred[16,6]{1,0:T(8,128)(4,1)S(1)} %copy.17), kind=kOutput, calls=%fused_computation.39 | convolution fusion | flops 944766976 | bytes 12058720 | tf_op jit(solution)/shard_map/iab,ibc->iac/dot_general | solution.py:46
  49.4 3.3 %gather_fusion.1 = bf16[32,128,256]{2,1,0:T(8,128)(2,1)} fusion(bf16[16,128,256]{2,1,0:T(8,128)(2,1)} %bitcast.124, s32[1024]{0:T(1024)S(1)} %pad_clamp_fusion), kind=kCustom, calls=%fused_computation.1.clone | custom fusion | bytes 4194432 | tf_op jit(solution)/shard_map/jit(_take)/gather | solution.py:49
  52.7 3.4 %fusion.90 = bf16[4,256,128]{1,2,0:T(8,128)(2,1)} fusion(bf16[4,128,128]{2,1,0:T(8,128)(2,1)S(1)} %copy-done.2, bf16[4,8,128,128]{3,2,1,0:T(8,128)(2,1)} %param.20, bf16[4,8,128,256]{3,2,1,0:T(8,128)(2,1)} %bitcast.134, pred[4,8]{1,0:T(4,128)(4,1)S(1)} %compare_and_fusion.1, bf16[4,128,256]{2,1,0:T(8,128)(2,1)} %bitcast.145), kind=kOutput, calls=%fused_computation.54 | convolution fusion | flops 303562752 | bytes 3801120 | tf_op jit(solution)/shard_map/jab,jbc->jac/dot_general | solution.py:57
  56.1 24.2 %all-gather.6.cloned.1.call-done = bf16[2048,256]{1,0:T(8,128)(2,1)} async-done(((bf16[512,256]{1,0:T(8,128)(2,1)}), bf16[2048,256]{1,0:T(8,128)(2,1)}) %all-gather.6.cloned.1.call-update) | async-done | bytes 1048592 | tf_op jit(solution)/shard_map/all_gather | solution.py:14
  80.3 3.2 %collective-permute-start = (bf16[2048,256]{1,0:T(8,128)(2,1)}, bf16[2048,256]{1,0:T(8,128)(2,1)}, u32[]{:S(2)}, u32[]{:S(2)}) collective-permute-start(bf16[2048,256]{1,0:T(8,128)(2,1)} %all-gather.6.cloned.1.call-done), channel_id=1, source_target_pairs={{0,4},{4,8},{8,12},{12,16},{16,20},{20,24},{24,28},{28,32},{32,36}... | collective-permute-start | bytes 3145736 | tf_op jit(solution)/shard_map/ppermute | solution.py:10
  83.5 28.4 %collective-permute-done = bf16[2048,256]{1,0:T(8,128)(2,1)} collective-permute-done((bf16[2048,256]{1,0:T(8,128)(2,1)}, bf16[2048,256]{1,0:T(8,128)(2,1)}, u32[]{:S(2)}, u32[]{:S(2)}) %collective-permute-start) | collective-permute-done | bytes 1048608 | tf_op jit(solution)/shard_map/ppermute | solution.py:10
  111.9 7.2 %gather_fusion.2 = bf16[96,128,256]{2,1,0:T(8,128)(2,1)} fusion(bf16[16,128,256]{2,1,0:T(8,128)(2,1)} %bitcast.16, s32[1024]{0:T(1024)S(1)} %pad_clamp_fusion.1), kind=kCustom, calls=%fused_computation.2.clone | custom fusion | bytes 12583296 | tf_op jit(solution)/shard_map/jit(_take)/gather | solution.py:38
  119.1 6.1 %fusion.42 = bf16[16,256,128]{1,2,0:T(8,128)(2,1)} fusion(bf16[16,128,128]{2,1,0:T(8,128)(2,1)} %param.18, bf16[16,128,256]{2,1,0:T(8,128)(2,1)} %bitcast.141, bf16[16,6,128,128]{3,2,1,0:T(8,128)(2,1)S(1)} %copy-done, bf16[16,6,128,256]{3,2,1,0:T(8,128)(2,1)} %bitcast.132, pred[16,6]{1,0:T(8,128)(4,1)S(1)} %copy.17), kind=kOutput, calls=%fused_computation.38 | convolution fusion | flops 944766976 | bytes 12058720 | tf_op jit(solution)/shard_map/iab,ibc->iac/dot_general | solution.py:46
  125.2 3.2 %gather_fusion.3 = bf16[32,128,256]{2,1,0:T(8,128)(2,1)} fusion(bf16[16,128,256]{2,1,0:T(8,128)(2,1)} %bitcast.126, s32[1024]{0:T(1024)S(1)} %pad_clamp_fusion), kind=kCustom, calls=%fused_computation.4.clone | custom fusion | bytes 4194432 | tf_op jit(solution)/shard_map/jit(_take)/gather | solution.py:49
  128.4 3.4 %fusion.87 = bf16[4,256,128]{1,2,0:T(8,128)(2,1)} fusion(bf16[4,128,128]{2,1,0:T(8,128)(2,1)S(1)} %copy-done.2, bf16[4,8,128,128]{3,2,1,0:T(8,128)(2,1)} %param.20, bf16[4,8,128,256]{3,2,1,0:T(8,128)(2,1)} %bitcast.135, pred[4,8]{1,0:T(4,128)(4,1)S(1)} %compare_and_fusion.1, bf16[4,128,256]{2,1,0:T(8,128)(2,1)S(1)} %bitcast.144), kind=kOutput, calls=%fused_computation.53 | convolution fusion | flops 303562752 | bytes 3801120 | tf_op jit(solution)/shard_map/jab,jbc->jac/dot_general | solution.py:57
  131.9 21.4 %all-gather.8.cloned.1.call-done = bf16[2048,256]{1,0:T(8,128)(2,1)} async-done(((bf16[512,256]{1,0:T(8,128)(2,1)}), bf16[2048,256]{1,0:T(8,128)(2,1)}) %all-gather.8.cloned.1.call-update) | async-done | bytes 1048592 | tf_op jit(solution)/shard_map/all_gather | solution.py:14
  153.3 3.4 %collective-permute-start.1 = (bf16[2048,256]{1,0:T(8,128)(2,1)}, bf16[2048,256]{1,0:T(8,128)(2,1)}, u32[]{:S(2)}, u32[]{:S(2)}) collective-permute-start(bf16[2048,256]{1,0:T(8,128)(2,1)} %all-gather.8.cloned.1.call-done), channel_id=1, source_target_pairs={{0,4},{4,8},{8,12},{12,16},{16,20},{20,24},{24,28},{28,32},{32,36}... | collective-permute-start | bytes 3145736 | tf_op jit(solution)/shard_map/ppermute | solution.py:10
  156.7 28.3 %collective-permute-done.1 = bf16[2048,256]{1,0:T(8,128)(2,1)} collective-permute-done((bf16[2048,256]{1,0:T(8,128)(2,1)}, bf16[2048,256]{1,0:T(8,128)(2,1)}, u32[]{:S(2)}, u32[]{:S(2)}) %collective-permute-start.1) | collective-permute-done | bytes 1048608 | tf_op jit(solution)/shard_map/ppermute | solution.py:10
  184.9 7.2 %gather_fusion.4 = bf16[96,128,256]{2,1,0:T(8,128)(2,1)} fusion(bf16[16,128,256]{2,1,0:T(8,128)(2,1)} %bitcast.31, s32[1024]{0:T(1024)S(1)} %pad_clamp_fusion.1), kind=kCustom, calls=%fused_computation.3.clone | custom fusion | bytes 12583296 | tf_op jit(solution)/shard_map/jit(_take)/gather | solution.py:38
  192.2 6.0 %fusion.39 = bf16[16,256,128]{1,2,0:T(8,128)(2,1)} fusion(bf16[16,128,128]{2,1,0:T(8,128)(2,1)} %param.18, bf16[16,128,256]{2,1,0:T(8,128)(2,1)} %bitcast.140, bf16[16,6,128,128]{3,2,1,0:T(8,128)(2,1)S(1)} %copy-done, bf16[16,6,128,256]{3,2,1,0:T(8,128)(2,1)} %bitcast.130, pred[16,6]{1,0:T(8,128)(4,1)S(1)} %copy.17), kind=kOutput, calls=%fused_computation.37 | convolution fusion | flops 944766976 | bytes 12058720 | tf_op jit(solution)/shard_map/iab,ibc->iac/dot_general | solution.py:46
  198.1 3.2 %gather_fusion.5 = bf16[32,128,256]{2,1,0:T(8,128)(2,1)} fusion(bf16[16,128,256]{2,1,0:T(8,128)(2,1)} %bitcast.128, s32[1024]{0:T(1024)S(1)} %pad_clamp_fusion), kind=kCustom, calls=%fused_computation.5.clone | custom fusion | bytes 4194432 | tf_op jit(solution)/shard_map/jit(_take)/gather | solution.py:49
  201.4 3.4 %fusion.84 = bf16[4,256,128]{1,2,0:T(8,128)(2,1)} fusion(bf16[4,128,128]{2,1,0:T(8,128)(2,1)S(1)} %copy-done.2, bf16[4,8,128,128]{3,2,1,0:T(8,128)(2,1)} %param.20, bf16[4,8,128,256]{3,2,1,0:T(8,128)(2,1)} %bitcast.133, pred[4,8]{1,0:T(4,128)(4,1)S(1)} %compare_and_fusion.1, bf16[4,128,256]{2,1,0:T(8,128)(2,1)} %bitcast.143), kind=kOutput, calls=%fused_computation.52 | convolution fusion | flops 303562752 | bytes 3801120 | tf_op jit(solution)/shard_map/jab,jbc->jac/dot_general | solution.py:57
  204.8 2.0 pad_maximum_fusion.1
  206.7 3.1 %pad_maximum_fusion = bf16[2048,768]{1,0:T(8,128)(2,1)} fusion(bf16[2048,256]{1,0:T(8,128)(2,1)} %bitcast.129, bf16[2048,256]{1,0:T(8,128)(2,1)} %bitcast.127, bf16[2048,256]{1,0:T(8,128)(2,1)} %bitcast.125), kind=kLoop, calls=%fused_computation.15 | loop fusion | flops 9437184 | bytes 6291456 | tf_op jit(solution)/shard_map/concatenate | solution.py:65
  (21 shorter events, 3.3 us)
Async XLA Ops:
  7.2 36.2 %copy-start = (bf16[16,6,128,128]{3,2,1,0:T(8,128)(2,1)S(1)}, bf16[16,6,128,128]{3,2,1,0:T(8,128)(2,1)}, u32[]{:S(2)}) copy-start(bf16[16,6,128,128]{3,2,1,0:T(8,128)(2,1)} %param.17) | copy-start | bytes 9437188
  7.2 29.0 %all-gather.4.cloned.1.call-start = ((), (), s32[]{:S(2)}) async-start(), calls=%async_computation | async-start | bytes 1310720 | tf_op jit(solution)/shard_map/all_gather | solution.py:14
  7.9 72.4 %all-gather.6.cloned.1.call-start = ((), (), s32[]{:S(2)}) async-start(), calls=%async_computation.1 | async-start | bytes 1310720 | tf_op jit(solution)/shard_map/all_gather | solution.py:14
  49.4 3.3 %copy-start.2 = (bf16[4,128,128]{2,1,0:T(8,128)(2,1)S(1)}, bf16[4,128,128]{2,1,0:T(8,128)(2,1)}, u32[]{:S(2)}) copy-start(bf16[4,128,128]{2,1,0:T(8,128)(2,1)} %param.21) | copy-start | bytes 393220
  56.1 97.2 %all-gather.8.cloned.1.call-start = ((), (), s32[]{:S(2)}) async-start(), calls=%async_computation.2 | async-start | bytes 1310720 | tf_op jit(solution)/shard_map/all_gather | solution.py:14
  80.3 31.6 %collective-permute-start = (bf16[2048,256]{1,0:T(8,128)(2,1)}, bf16[2048,256]{1,0:T(8,128)(2,1)}, u32[]{:S(2)}, u32[]{:S(2)}) collective-permute-start(bf16[2048,256]{1,0:T(8,128)(2,1)} %all-gather.6.cloned.1.call-done), channel_id=1, source_target_pairs={{0,4},{4,8},{8,12},{12,16},{16,20},{20,24},{24,28},{28,32},{32,36}... | collective-permute-start | bytes 3145736 | tf_op jit(solution)/shard_map/ppermute | solution.py:10
  153.3 31.6 %collective-permute-start.1 = (bf16[2048,256]{1,0:T(8,128)(2,1)}, bf16[2048,256]{1,0:T(8,128)(2,1)}, u32[]{:S(2)}, u32[]{:S(2)}) collective-permute-start(bf16[2048,256]{1,0:T(8,128)(2,1)} %all-gather.8.cloned.1.call-done), channel_id=1, source_target_pairs={{0,4},{4,8},{8,12},{12,16},{16,20},{20,24},{24,28},{28,32},{32,36}... | collective-permute-start | bytes 3145736 | tf_op jit(solution)/shard_map/ppermute | solution.py:10
  201.4 3.4 %copy-start.1 = (bf16[4,256,128]{1,2,0:T(8,128)(2,1)S(1)}, bf16[4,256,128]{1,2,0:T(8,128)(2,1)}, u32[]{:S(2)}) copy-start(bf16[4,256,128]{1,2,0:T(8,128)(2,1)} %fusion.90) | copy-start | bytes 786436
Sparse Core Ops, SparseCore 0:
  9.8 26.2 all-gather.3
  56.2 24.0 all-gather.5
  132.0 21.2 all-gather.7
where the time goes:
time: 217 us; the launch traced here: 216 us
  waiting for transfers between devices  122 us (56%)
  local copies, waits for them, and re-layouts  37.3 us (17%)
  matrix products  28.3 us (13%)
  between operations  13.8 us (6%)
  other arithmetic  8.01 us (4%)
  starting transfers between devices  6.64 us (3%)
    all_gather x3, waiting for transfers between devices, collect(): return lax.all_gather(share, 'sub', axis=0, tiled=True)  64.9 us
    ppermute x2, waiting for transfers between devices, passed_along(): return lax.ppermute(x, axis, pairs)  56.7 us
    gather x3, local copies, waits for them, and re-layouts, shards(): picked = jnp.take(front_blocks, inner_index, axis=0)  21.7 us
    dot_general x3, matrix products, shards(): jnp.einsum('iab,ibc->iac', inner_inverse, inner_values, preferred_element...  18.1 us
    dot_general x3, matrix products, shards(): jnp.einsum('jab,jbc->jac', front_inverse, outer_values, preferred_element...  10.2 us
    gather x3, local copies, waits for them, and re-layouts, shards(): chosen = jnp.take(solved, outer_index, axis=0)  9.7 us
    ppermute x2, starting transfers between devices, passed_along(): return lax.ppermute(x, axis, pairs)  6.53 us
  transfers between devices with their start and end apart: 5, of which 5 were waited for; matrix products, arithmetic and copies ran while one was open for 4% of the time, Pallas kernels for 0%

commit v1 on v0

v1 whole, which is shorter than its diff:
```python
import jax
import jax.numpy as jnp
from jax import lax
from jax.experimental import pallas as pl
from jax.experimental.pallas import tpu as pltpu
from jax.sharding import PartitionSpec as P

BF = jnp.bfloat16
F32 = jnp.float32
MESH = pl.DeviceIdType.MESH
BL = 128
NI = 16
NL = 6
NJ = 4
NK = 8
NF = 16
NT = 3
CW = 256
HW = 128


def lanes(parts):
    return jnp.concatenate(parts, axis=1)


def rows(parts):
    return jnp.concatenate(parts, axis=0)


def mm(a, b):
    return jnp.dot(a, b, preferred_element_type=F32)


def kernel(
    n_slab,
    iidx,
    oidx,
    rhs_h,
    front_h,
    pend_h,
    a_h,
    inv_h,
    b_h,
    finv_h,
    sol_h,
    fro_h,
    f00,
    f01,
    f10,
    f11,
    f20,
    f21,
    a,
    inv,
    b,
    finv,
    rhs,
    front,
    p32,
    pbf,
    cmat,
    w,
    y,
    ysend,
    s,
    pos,
    load_sem,
    out_sem,
    send_z,
    recv_z,
    send_s,
    recv_s,
    send_x,
    recv_x,
    send_xs,
    recv_xs,
):
    fr = ((f00, f01), (f10, f11), (f20, f21))
    slab = lax.axis_index("slab")
    sub = lax.axis_index("sub")
    sib = sub + 1 - 2 * (sub % 2)
    xp = (sub + 2) % 4
    crossed_out = ((slab + 1) % 8 == 0).astype(jnp.int32)
    crossed_in = (slab % 8 == 0).astype(jnp.int32)
    nxt = (slab + 1) % n_slab
    prv = (slab + n_slab - 1) % n_slab
    to_sub = (sub + 2 * crossed_out) % 4
    from_sub = (sub + 2 * crossed_in) % 4
    last = slab == n_slab - 1

    sib_id = (slab, sib)
    x_id = (slab, xp)
    next_id = (nxt, to_sub)
    prev_id = (prv, from_sub)

    barrier = pltpu.get_barrier_semaphore()
    for peer in (sib_id, x_id, next_id, prev_id):
        pl.semaphore_signal(barrier, inc=1, device_id=peer, device_id_type=MESH)

    def share(t):
        base = sub if t == 0 else from_sub
        one = base + 1 - 2 * (base % 2)
        return (base, one, (base + 2) % 4, (one + 2) % 4)

    loads = []

    def load(src, dst):
        copy = pltpu.make_async_copy(src, dst, load_sem.at[len(loads)])
        copy.start()
        loads.append(copy)
        return copy

    own = [
        [
            load(
                pend_h.at[:, :, c * HW : (c + 1) * HW],
                fr[0][c].at[pl.ds(4 * sub, 4)],
            )
            for c in range(1)
        ]
    ][0]
    ld_inv = load(inv_h, inv)
    ld_a = [
        load(a_h.at[pl.ds(4 * g, 4)], a.at[pl.ds(4 * g, 4), pl.ds(0, NL)])
        for g in range(4)
    ]
    ld_finv = load(finv_h, finv)
    ld_b = load(b_h, b)
    own.append(load(pend_h.at[:, :, HW:CW], fr[0][1].at[pl.ds(4 * sub, 4)]))
    ld_r = [load(rhs_h.at[:, :, 0:CW], rhs.at[0])]
    ld_g = load(front_h, front)
    for t in range(1, NT):
        ld_r.append(load(rhs_h.at[:, :, t * CW : (t + 1) * CW], rhs.at[t]))

    sends = []

    def send(src, dst, ssem, rsem, peer):
        copy = pltpu.make_async_remote_copy(
            src_ref=src,
            dst_ref=dst,
            send_sem=ssem,
            recv_sem=rsem,
            device_id=peer,
            device_id_type=MESH,
        )
        copy.start()
        sends.append(copy)

    def arrival(t, c, which, p, rsem):
        block = fr[t][c].at[4 * share(t)[which] + p]
        return pltpu.make_async_copy(block, block, rsem.at[t, c, p])

    pl.semaphore_wait(barrier, 4)

    base0 = share(0)[0]
    for c in range(2):
        for p in range(NJ):
            src = pend_h.at[p, :, c * HW : (c + 1) * HW]
            dst = fr[0][c].at[4 * base0 + p]
            send(src, dst, send_x.at[0, c, p], recv_x.at[0, c, p], x_id)
            send(src, dst, send_s.at[0, c, p], recv_s.at[0, c, p], sib_id)

    def fwd_z(t, c, p):
        arrival(t, c, 0, p, recv_z).wait()
        block = fr[t][c].at[4 * share(t)[0] + p]
        send(block, block, send_x.at[t, c, p], recv_x.at[t, c, p], x_id)
        send(block, block, send_s.at[t, c, p], recv_s.at[t, c, p], sib_id)

    def fwd_x(t, c, p):
        arrival(t, c, 2, p, recv_x).wait()
        block = fr[t][c].at[4 * share(t)[2] + p]
        send(block, block, send_xs.at[t, c, p], recv_xs.at[t, c, p], sib_id)

    def place(i, carry):
        own_links = [iidx[i, k] for k in range(NL)]
        for f in range(NF):
            at = jnp.int32(NL)
            for k in range(NL):
                at = jnp.where(own_links[k] == f, jnp.int32(k), at)
            pos[i * NF + f] = at
        return carry

    lax.fori_loop(0, NI, place, 0)

    for i in range(NI):
        a[i, NL] = jnp.zeros((BL, BL), BF)

    ld_inv.wait()
    for g in range(4):
        ld_a[g].wait()
        for i in range(4 * g, 4 * g + 4):
            for m in range(0, NL, 2):
                o = mm(inv[i], lanes([a[i, m], a[i, m + 1]]))
                o = (-o).astype(BF)
                a[i, m] = o[:, :BL]
                a[i, m + 1] = o[:, BL:]

    ld_finv.wait()
    ld_b.wait()
    for j in range(NJ):
        for m in range(0, NK, 2):
            o = mm(finv[j], lanes([b[j, m], b[j, m + 1]]))
            o = (-o).astype(BF)
            b[j, m] = o[:, :BL]
            b[j, m + 1] = o[:, BL:]

    def c_step(g):
        for j in range(NJ):
            tiles = []
            for k in range(NK):
                at = oidx[j, k]
                tiles.append(
                    lanes(
                        [
                            a[at, pos[at * NF + 2 * g]],
                            a[at, pos[at * NF + 2 * g + 1]],
                        ]
                    )
                )
            o = mm(lanes([b[j, k] for k in range(NK)]), rows(tiles)).astype(BF)
            cmat[2 * g, pl.ds(j * BL, BL)] = o[:, :BL]
            cmat[2 * g + 1, pl.ds(j * BL, BL)] = o[:, BL:]

    for g in range(NF // 2):
        c_step(g)
        if g in (2, 4, 6):
            fwd_x(0, 0, g // 2 - 1)

    def p_step(t):
        ld_r[t].wait()
        for i in range(NI):
            o = mm(inv[i], rhs[t, i])
            p32[t, i] = o
            pbf[t, i] = o.astype(BF)

    def w_step(t):
        if t == 0:
            ld_g.wait()
        for j in range(NJ):
            left = lanes([finv[j]] + [b[j, k] for k in range(NK)])
            right = rows(
                [front[j, :, t * CW : (t + 1) * CW]]
                + [pbf[t, oidx[j, k]] for k in range(NK)]
            )
            o = mm(left, right)
            w[t, 0, pl.ds(j * BL, BL)] = o[:, :HW]
            w[t, 1, pl.ds(j * BL, BL)] = o[:, HW:]

    def acc(t, c, which):
        sh = share(t)[which]
        if which == 0 and t == 0:
            own[c].wait()
        elif which == 1:
            for p in range(NJ):
                arrival(t, c, 1, p, recv_s).wait()
        elif which == 3:
            for p in range(NJ):
                arrival(t, c, 3, p, recv_xs).wait()
        left = lanes([cmat[4 * sh + r] for r in range(4)])
        right = fr[t][c][pl.ds(4 * sh, 4)].reshape(4 * BL, HW)
        w[t, c] = w[t, c] + mm(left, right)

    outs = []

    def put(src, dst):
        copy = pltpu.make_async_copy(src, dst, out_sem.at[len(outs)])
        copy.start()
        outs.append(copy)

    def y_step(t, c):
        value = w[t, c].astype(BF)
        if t + 1 < NT:
            passed = jnp.where(last, jnp.zeros_like(value), value)
            ysend[t, c] = passed.reshape(NJ, BL, HW)
            for p in range(NJ):
                send(
                    ysend.at[t, c, p],
                    fr[t + 1][c].at[4 * sub + p],
                    send_z.at[t + 1, c, p],
                    recv_z.at[t + 1, c, p],
                    next_id,
                )
        y[t, c] = value.reshape(NJ, BL, HW)
        at = t * CW + c * HW
        put(y.at[t, c], fro_h.at[:, :, at : at + HW])

    def s_step(t, g):
        for i in range(4 * g, 4 * g + 4):
            left = lanes([a[i, k] for k in range(NL)])
            right = rows(
                [
                    lanes([fr[t][0][iidx[i, k]], fr[t][1][iidx[i, k]]])
                    for k in range(NL)
                ]
            )
            s[t, i] = (p32[t, i] + mm(left, right)).astype(BF)
        put(
            s.at[t, pl.ds(4 * g, 4)],
            sol_h.at[pl.ds(4 * g, 4), :, t * CW : (t + 1) * CW],
        )

    p_step(0)
    fwd_x(0, 0, 3)
    w_step(0)
    fwd_x(0, 1, 0)
    for which in range(4):
        acc(0, 0, which)
    y_step(0, 0)
    fwd_x(0, 1, 1)
    p_step(1)
    fwd_x(0, 1, 2)
    acc(0, 1, 0)
    acc(0, 1, 1)
    fwd_x(0, 1, 3)
    w_step(1)
    acc(0, 1, 2)
    acc(0, 1, 3)
    y_step(0, 1)

    for t in range(NT - 1):
        n = t + 1
        for p in range(NJ):
            fwd_z(n, 0, p)
            s_step(t, p)
        if n + 1 < NT:
            p_step(n + 1)
            fwd_x(n, 0, 0)
            fwd_z(n, 1, 0)
            w_step(n + 1)
        else:
            fwd_x(n, 0, 0)
            fwd_z(n, 1, 0)
        acc(n, 0, 0)
        fwd_x(n, 0, 1)
        fwd_z(n, 1, 1)
        acc(n, 0, 1)
        fwd_x(n, 0, 2)
        fwd_z(n, 1, 2)
        fwd_x(n, 0, 3)
        fwd_z(n, 1, 3)
        acc(n, 0, 2)
        fwd_x(n, 1, 0)
        acc(n, 0, 3)
        y_step(n, 0)
        fwd_x(n, 1, 1)
        acc(n, 1, 0)
        fwd_x(n, 1, 2)
        acc(n, 1, 1)
        fwd_x(n, 1, 3)
        acc(n, 1, 2)
        acc(n, 1, 3)
        y_step(n, 1)

    for g in range(4):
        s_step(NT - 1, g)

    for copy in sends:
        copy.wait_send()
    for copy in outs:
        copy.wait()


def solution(mesh):
    n_slab = mesh.shape["slab"]

    def shards(rhs, front, pend, iidx, a, inv, oidx, b, finv):
        smem = pl.BlockSpec(memory_space=pltpu.SMEM)
        anyw = pl.BlockSpec(memory_space=pl.ANY)
        dma = pltpu.SemaphoreType.DMA
        half = pltpu.VMEM((NF, BL, HW), BF)
        sol, fro = pl.pallas_call(
            lambda *refs: kernel(n_slab, *refs),
            name="substitution",
            out_shape=(
                jax.ShapeDtypeStruct((NI, BL, NT * CW), BF),
                jax.ShapeDtypeStruct((NJ, BL, NT * CW), BF),
            ),
            in_specs=[smem, smem] + [anyw] * 7,
            out_specs=(anyw, anyw),
            scratch_shapes=[half] * 6
            + [
                pltpu.VMEM((NI, NL + 1, BL, BL), BF),
                pltpu.VMEM((NI, BL, BL), BF),
                pltpu.VMEM((NJ, NK, BL, BL), BF),
                pltpu.VMEM((NJ, BL, BL), BF),
                pltpu.VMEM((NT, NI, BL, CW), BF),
                pltpu.VMEM((NJ, BL, NT * CW), BF),
                pltpu.VMEM((NT, NI, BL, CW), F32),
                pltpu.VMEM((NT, NI, BL, CW), BF),
                pltpu.VMEM((NF, NJ * BL, BL), BF),
                pltpu.VMEM((NT, 2, NJ * BL, HW), F32),
                pltpu.VMEM((NT, 2, NJ, BL, HW), BF),
                pltpu.VMEM((NT - 1, 2, NJ, BL, HW), BF),
                pltpu.VMEM((NT, NI, BL, CW), BF),
                pltpu.SMEM((NI * NF,), jnp.int32),
                dma((16,)),
                dma((32,)),
            ]
            + [dma((NT, 2, NJ))] * 8,
            compiler_params=pltpu.CompilerParams(
                collective_id=0,
                has_side_effects=True,
                vmem_limit_bytes=56 * 1024 * 1024,
            ),
        )(
            iidx,
            oidx,
            rhs.reshape(NI, BL, NT * CW),
            front.reshape(NJ, BL, NT * CW),
            pend.reshape(NJ, BL, CW),
            a,
            inv,
            b,
            finv,
        )
        return sol.reshape(NI * BL, NT * CW), fro.reshape(NJ * BL, NT * CW)

    both = ("slab", "sub")
    two = P(both, None)
    return jax.shard_map(
        shards,
        mesh=mesh,
        in_specs=(
            two,
            two,
            two,
            two,
            P(both, None, None, None),
            P(both, None, None),
            two,
            P(both, None, None, None),
            P(both, None, None),
        ),
        out_specs=(two, two),
        check_vma=False,
    )
```

time: 217 us -> 53.7 us (0.25)
  the two profiles are of different devices: /device:TPU:25 before, /device:TPU:1 now
where the time goes in v1:
time: 53.7 us; the launch traced here: 53.5 us
  Pallas kernels  46.8 us (87%)
  local copies, waits for them, and re-layouts  6.07 us (11%)
  between operations  0.65 us (1%)
    pallas_call x1, Pallas kernels, shards(): pl.pallas_call(lambda *refs: kernel(n_slab, *refs), name='substitution',...  46.8 us
    unnamed x5, local copies, waits for them, and re-layouts  6.07 us

profile of v1, /device:TPU:1, one launch (start us, length us, event | category | flops | bytes accessed | tf_op | source)
XLA Modules:
  0.0 53.5 jit_solution(15933107221888354174)
XLA Ops:
  0.6 1.4 %copy.11.refs_0_ = s32[16,6]{1,0:T(8,128)} copy(s32[16,6]{0,1:T(8,128)} %param.12) | data formatting | bytes 768 | tf_op args[3]
  2.0 46.8 %substitution.1 = (bf16[16,128,768]{2,1,0:T(8,128)(2,1)}, bf16[4,128,768]{2,1,0:T(8,128)(2,1)}) custom-call(s32[16,6]{1,0:T(8,128)} %copy.11.refs_0_, s32[4,8]{1,0:T(4,128)} %refs_1_.1, bf16[16,128,768]{2,1,0:T(8,128)(2,1)} %bitcast.5, bf16[4,128,768]{2,1,0:T(8,128)(2,1)} %bitcast.7, bf16[4,128,256]{2,1,0:T(8,128)(2,1)} %bitcast.9, ...), custom_call_target="tpu_custom_call" | custom-call | tf_op jit(solution)/shard_map/substitution/pallas_call | solution.py:371
  48.8 0.0 copy-start
  48.8 3.8 %copy.14 = bf16[2048,768]{1,0:T(8,128)(2,1)} copy(bf16[2048,768]{1,0:T(8,128)(2,1)} %bitcast.6) | data formatting | bytes 6291456
  52.6 0.0 copy-done
  52.6 0.9 %copy.15 = bf16[512,768]{1,0:T(8,128)(2,1)} copy(bf16[512,768]{1,0:T(8,128)(2,1)S(1)} %bitcast.8) | data formatting | bytes 1572864
Async XLA Ops:
  48.8 3.8 %copy-start = (bf16[4,128,768]{2,1,0:T(8,128)(2,1)S(1)}, bf16[4,128,768]{2,1,0:T(8,128)(2,1)}, u32[]{:S(2)}) copy-start(bf16[4,128,768]{2,1,0:T(8,128)(2,1)} %get-tuple-element.5) | copy-start | bytes 2359300

commit v2 on v1

v2 whole, which is shorter than its diff:
```python
import jax
import jax.numpy as jnp
from jax import lax
from jax.experimental import pallas as pl
from jax.experimental.pallas import tpu as pltpu
from jax.sharding import PartitionSpec as P

BF = jnp.bfloat16
F32 = jnp.float32
MESH = pl.DeviceIdType.MESH
BL = 128
NI = 16
NL = 6
NJ = 4
NK = 8
NF = 16
NT = 3
CW = 256
HW = 128


def lanes(parts):
    return jnp.concatenate(parts, axis=1)


def rows(parts):
    return jnp.concatenate(parts, axis=0)


def mm(a, b):
    return jnp.dot(a, b, preferred_element_type=F32)


def kernel(
    n_slab,
    iidx_h,
    oidx_h,
    rhs_h,
    front_h,
    pend_h,
    a_h,
    inv_h,
    b_h,
    finv_h,
    sol,
    fro,
    f00,
    f01,
    f10,
    f11,
    f20,
    f21,
    a,
    inv,
    b,
    finv,
    rhs,
    front,
    p32,
    pbf,
    cmat,
    w,
    ysend,
    iidx,
    oidx,
    pos,
    load_sem,
    send_z,
    recv_z,
    send_s,
    recv_s,
    send_x,
    recv_x,
    send_xs,
    recv_xs,
):
    fr = ((f00, f01), (f10, f11), (f20, f21))
    slab = lax.axis_index("slab")
    sub = lax.axis_index("sub")
    sib = sub + 1 - 2 * (sub % 2)
    xp = (sub + 2) % 4
    to_sub = (sub + 2 * ((slab + 1) % 8 == 0).astype(jnp.int32)) % 4
    from_sub = (sub + 2 * (slab % 8 == 0).astype(jnp.int32)) % 4
    gives = slab < n_slab - 1
    takes = slab > 0
    sib_id = (slab, sib)
    x_id = (slab, xp)
    next_id = ((slab + 1) % n_slab, to_sub)
    prev_id = ((slab + n_slab - 1) % n_slab, from_sub)

    barrier = pltpu.get_barrier_semaphore()
    for peer in (sib_id, x_id):
        pl.semaphore_signal(barrier, inc=1, device_id=peer, device_id_type=MESH)

    @pl.when(takes)
    def _():
        pl.semaphore_signal(barrier, inc=1, device_id=prev_id, device_id_type=MESH)

    def share(t):
        base = sub if t == 0 else from_sub
        one = base + 1 - 2 * (base % 2)
        return (base, one, (base + 2) % 4, (one + 2) % 4)

    loads = []

    def load(src, dst):
        copy = pltpu.make_async_copy(src, dst, load_sem.at[len(loads)])
        copy.start()
        loads.append(copy)
        return copy

    ld_idx = [load(iidx_h, iidx), load(oidx_h, oidx)]
    ld_inv = load(inv_h, inv)
    ld_a = [
        load(a_h.at[pl.ds(4 * g, 4)], a.at[pl.ds(4 * g, 4), pl.ds(0, NL)])
        for g in range(4)
    ]
    ld_finv = load(finv_h, finv)
    ld_b = load(b_h, b)
    ld_r = [load(rhs_h.at[:, :, 0:CW], rhs.at[0])]
    own = [
        load(
            pend_h.at[:, :, c * HW : (c + 1) * HW],
            fr[0][c].at[pl.ds(4 * sub, 4)],
        )
        for c in range(2)
    ]
    ld_g = load(front_h, front)
    for t in range(1, NT):
        ld_r.append(load(rhs_h.at[:, :, t * CW : (t + 1) * CW], rhs.at[t]))

    sends = []

    def send(when, src, dst, ssem, rsem, ssem_at, peer):
        copy = pltpu.make_async_remote_copy(
            src_ref=src,
            dst_ref=dst,
            send_sem=ssem.at[ssem_at],
            recv_sem=rsem.at[ssem_at],
            device_id=peer,
            device_id_type=MESH,
        )
        copy.start()
        sends.append((when, ssem, ssem_at))

    def gated(when, body):
        if when is None:
            body()
        else:
            pl.when(when)(body)

    def taken(t):
        return takes if t else None

    def arrived(t, c, which, p, rsem):
        block = fr[t][c].at[4 * share(t)[which] + p]
        pltpu.make_async_copy(block, block, rsem.at[t, c, p]).wait()

    def greet():
        pl.semaphore_wait(barrier, 2 + gives.astype(jnp.int32))

    def gather():
        for c in range(2):
            for p in range(NJ):
                src = pend_h.at[p, :, c * HW : (c + 1) * HW]
                dst = fr[0][c].at[4 * share(0)[0] + p]
                send(None, src, dst, send_x, recv_x, (0, c, p), x_id)
            for p in range(NJ):
                src = pend_h.at[p, :, c * HW : (c + 1) * HW]
                dst = fr[0][c].at[4 * share(0)[0] + p]
                send(None, src, dst, send_s, recv_s, (0, c, p), sib_id)

    def fwd_z(t, c, *ps):
        def body():
            for p in ps:
                arrived(t, c, 0, p, recv_z)
                block = fr[t][c].at[4 * share(t)[0] + p]
                at = (t, c, p)
                send(takes, block, block, send_x, recv_x, at, x_id)
                send(takes, block, block, send_s, recv_s, at, sib_id)

        gated(taken(t), body)

    def fwd_x(t, c, *ps):
        def body():
            for p in ps:
                arrived(t, c, 2, p, recv_x)
                block = fr[t][c].at[4 * share(t)[2] + p]
                at = (t, c, p)
                send(taken(t), block, block, send_xs, recv_xs, at, sib_id)

        gated(taken(t), body)

    def arr_s(t, c):
        def body():
            for p in range(NJ):
                arrived(t, c, 1, p, recv_s)

        gated(taken(t), body)

    def arr_xs(t, c):
        def body():
            for p in range(NJ):
                arrived(t, c, 3, p, recv_xs)

        gated(taken(t), body)

    def place(i, carry):
        own_links = [iidx[k, i] for k in range(NL)]
        for f in range(NF):
            at = jnp.int32(NL)
            for k in range(NL):
                at = jnp.where(own_links[k] == f, jnp.int32(k), at)
            pos[i * NF + f] = at
        return carry

    def places():
        for copy in ld_idx:
            copy.wait()
        lax.fori_loop(0, NI, place, 0)
        for i in range(NI):
            a[i, NL] = jnp.zeros((BL, BL), BF)

        @pl.when(slab == 0)
        def _():
            for t in range(1, NT):
                for c in range(2):
                    fr[t][c][...] = jnp.zeros((NF, BL, HW), BF)

    def a_wait(g):
        if g == 0:
            ld_inv.wait()
        ld_a[g].wait()

    def a_step(g):
        for i in range(4 * g, 4 * g + 4):
            for m in range(0, NL, 2):
                o = mm(inv[i], lanes([a[i, m], a[i, m + 1]]))
                o = (-o).astype(BF)
                a[i, m] = o[:, :BL]
                a[i, m + 1] = o[:, BL:]

    def b_wait():
        ld_finv.wait()
        ld_b.wait()

    def b_step():
        for j in range(NJ):
            for m in range(0, NK, 2):
                o = mm(finv[j], lanes([b[j, m], b[j, m + 1]]))
                o = (-o).astype(BF)
                b[j, m] = o[:, :BL]
                b[j, m + 1] = o[:, BL:]

    def c_step(*gs):
        for g in gs:
            for j in range(NJ):
                tiles = []
                for k in range(NK):
                    at = oidx[j, k]
                    tiles.append(
                        lanes(
                            [
                                a[at, pos[at * NF + 2 * g]],
                                a[at, pos[at * NF + 2 * g + 1]],
                            ]
                        )
                    )
                o = mm(lanes([b[j, k] for k in range(NK)]), rows(tiles)).astype(BF)
                cmat[2 * g, pl.ds(j * BL, BL)] = o[:, :BL]
                cmat[2 * g + 1, pl.ds(j * BL, BL)] = o[:, BL:]

    def p_step(t):
        ld_r[t].wait()
        for i in range(NI):
            o = mm(inv[i], rhs[t, i])
            p32[t, i] = o
            if t:
                pbf[t - 1, i] = o.astype(BF)

    def front_left(j):
        return lanes([finv[j]] + [b[j, k] for k in range(NK)])

    def w_step(t):
        for j in range(NJ):
            right = rows(
                [front[j, :, t * CW : (t + 1) * CW]]
                + [pbf[t - 1, oidx[j, k]] for k in range(NK)]
            )
            o = mm(front_left(j), right)
            w[t - 1, 0, pl.ds(j * BL, BL)] = o[:, :HW]
            w[t - 1, 1, pl.ds(j * BL, BL)] = o[:, HW:]

    def acc(t, c, *which):
        shares = [share(t)[n] for n in which]
        left = lanes([cmat[4 * sh + r] for sh in shares for r in range(4)])
        right = rows([fr[t][c][pl.ds(4 * sh, 4)].reshape(4 * BL, HW) for sh in shares])
        return w[t - 1, c] + mm(left, right)

    def acc3(t, c):
        arr_s(t, c)
        w[t - 1, c] = acc(t, c, 0, 1, 2)

    def pass_on(t, c):
        def body():
            for p in range(NJ):
                at = (t + 1, c, p)
                send(
                    gives,
                    ysend.at[t, c, p],
                    fr[t + 1][c].at[4 * sub + p],
                    send_z,
                    recv_z,
                    at,
                    next_id,
                )

        gated(gives, body)

    def columns(t, c):
        return slice(t * CW + c * HW, t * CW + (c + 1) * HW)

    def y_step(t, c):
        arr_xs(t, c)
        value = acc(t, c, 3).astype(BF).reshape(NJ, BL, HW)
        if t + 1 < NT:
            ysend[t, c] = value
            pass_on(t, c)
        fro[:, :, columns(t, c)] = value

    def s0_wait(c):
        own[c].wait()
        arr_s(0, c)
        arr_xs(0, c)

    def s0_step(c, *ids):
        for i in ids:
            left = lanes([a[i, k] for k in range(NL)])
            right = rows([fr[0][c][iidx[k, i]] for k in range(NL)])
            base = p32[0, i, :, c * HW : (c + 1) * HW]
            sol[i, :, columns(0, c)] = (base + mm(left, right)).astype(BF)

    def y0_step(c):
        for j in range(NJ):
            right = rows(
                [front[j, :, columns(0, c)]]
                + [sol[oidx[j, k], :, columns(0, c)] for k in range(NK)]
            )
            value = mm(front_left(j), right).astype(BF)
            ysend[0, c, j] = value
            fro[j, :, columns(0, c)] = value
        pass_on(0, c)

    def s_step(t, *ids):
        for i in ids:
            left = lanes([a[i, k] for k in range(NL)])
            right = rows(
                [
                    lanes([fr[t][0][iidx[k, i]], fr[t][1][iidx[k, i]]])
                    for k in range(NL)
                ]
            )
            o = (p32[t, i] + mm(left, right)).astype(BF)
            sol[i, :, t * CW : (t + 1) * CW] = o

    places()
    greet()
    gather()
    for g in range(4):
        a_wait(g)
        a_step(g)
    b_wait()
    b_step()
    p_step(0)
    fwd_x(0, 0, 0)
    c_step(0)
    fwd_x(0, 0, 1)
    c_step(1)
    fwd_x(0, 0, 2, 3)
    c_step(2)
    fwd_x(0, 1, 0)
    s0_wait(0)
    s0_step(0, *range(0, 8))
    fwd_x(0, 1, 1, 2)
    s0_step(0, *range(8, 16))
    fwd_x(0, 1, 3)
    ld_g.wait()
    y0_step(0)
    s0_wait(1)
    s0_step(1, *range(16))
    y0_step(1)
    c_step(3, 4)
    fwd_z(1, 0, 0, 1)
    c_step(5)
    fwd_z(1, 0, 2, 3)
    c_step(6)
    fwd_z(1, 1, 0, 1)
    c_step(7)
    fwd_z(1, 1, 2)
    p_step(1)
    fwd_z(1, 1, 3)
    fwd_x(1, 0, 0, 1)
    w_step(1)
    fwd_x(1, 0, 2, 3)
    acc3(1, 0)
    fwd_x(1, 1, 0)
    y_step(1, 0)
    fwd_x(1, 1, 1, 2, 3)
    acc3(1, 1)
    y_step(1, 1)
    s_step(1, *range(0, 8))
    fwd_z(2, 0, 0, 1)
    s_step(1, *range(8, 12))
    fwd_z(2, 0, 2, 3)
    s_step(1, *range(12, 16))
    fwd_z(2, 1, 0, 1)
    p_step(2)
    fwd_z(2, 1, 2, 3)
    w_step(2)
    fwd_x(2, 0, 0, 1, 2, 3)
    acc3(2, 0)
    fwd_x(2, 1, 0)
    y_step(2, 0)
    fwd_x(2, 1, 1, 2, 3)
    acc3(2, 1)
    y_step(2, 1)
    s_step(2, *range(16))

    def finish():
        for when in (None, takes, gives):
            sent = [(sem, at) for cond, sem, at in sends if cond is when]

            def body(sent=sent):
                for sem, at in sent:
                    block = ysend.at[0, 0, 0]
                    pltpu.make_async_copy(block, block, sem.at[at]).wait()

            gated(when, body)

    finish()


def solution(mesh):
    n_slab = mesh.shape["slab"]

    def shards(rhs, front, pend, iidx, a, inv, oidx, b, finv):
        vmem = pl.BlockSpec(memory_space=pltpu.VMEM)
        hbm = pl.BlockSpec(memory_space=pltpu.HBM)
        dma = pltpu.SemaphoreType.DMA
        half = pltpu.VMEM((NF, BL, HW), BF)
        sol, fro = pl.pallas_call(
            lambda *refs: kernel(n_slab, *refs),
            name="substitution",
            out_shape=(
                pltpu.VMEM((NI, BL, NT * CW), BF),
                pltpu.VMEM((NJ, BL, NT * CW), BF),
            ),
            in_specs=[hbm] * 9,
            out_specs=(vmem, vmem),
            scratch_shapes=[half] * 6
            + [
                pltpu.VMEM((NI, NL + 1, BL, BL), BF),
                pltpu.VMEM((NI, BL, BL), BF),
                pltpu.VMEM((NJ, NK, BL, BL), BF),
                pltpu.VMEM((NJ, BL, BL), BF),
                pltpu.VMEM((NT, NI, BL, CW), BF),
                pltpu.VMEM((NJ, BL, NT * CW), BF),
                pltpu.VMEM((NT, NI, BL, CW), F32),
                pltpu.VMEM((NT - 1, NI, BL, CW), BF),
                pltpu.VMEM((NF, NJ * BL, BL), BF),
                pltpu.VMEM((NT - 1, 2, NJ * BL, HW), F32),
                pltpu.VMEM((NT - 1, 2, NJ, BL, HW), BF),
                pltpu.SMEM((NL, NI), jnp.int32),
                pltpu.SMEM((NJ, NK), jnp.int32),
                pltpu.SMEM((NI * NF,), jnp.int32),
                dma((16,)),
            ]
            + [dma((NT, 2, NJ))] * 8,
            compiler_params=pltpu.CompilerParams(
                collective_id=0,
                has_side_effects=True,
                vmem_limit_bytes=36 * 1024 * 1024,
            ),
        )(
            *(
                pltpu.with_memory_space_constraint(x, pltpu.HBM)
                for x in (
                    iidx.T,
                    oidx,
                    rhs.reshape(NI, BL, NT * CW),
                    front.reshape(NJ, BL, NT * CW),
                    pend.reshape(NJ, BL, CW),
                    a,
                    inv,
                    b,
                    finv,
                )
            )
        )
        return sol.reshape(NI * BL, NT * CW), fro.reshape(NJ * BL, NT * CW)

    both = ("slab", "sub")
    two = P(both, None)
    return jax.shard_map(
        shards,
        mesh=mesh,
        in_specs=(
            two,
            two,
            two,
            two,
            P(both, None, None, None),
            P(both, None, None),
            two,
            P(both, None, None, None),
            P(both, None, None),
        ),
        out_specs=(two, two),
        check_vma=False,
    )
```

time: 53.7 us -> 45.9 us (0.85)
  the two profiles are of different devices: /device:TPU:1 before, /device:TPU:25 now
where the time goes in v2:
time: 45.9 us; the launch traced here: 45.8 us
  Pallas kernels  42.6 us (93%)
  local copies, waits for them, and re-layouts  2.55 us (6%)
  between operations  0.64 us (1%)
    pallas_call x1, Pallas kernels, shards(): pl.pallas_call(lambda *refs: kernel(n_slab, *refs), name='substitution',...  42.6 us
    unnamed x2, local copies, waits for them, and re-layouts  2.55 us

profile of v2, /device:TPU:25, one launch (start us, length us, event | category | flops | bytes accessed | tf_op | source)
XLA Modules:
  0.0 45.8 jit_solution(10433145861117297728)
XLA Ops:
  0.6 42.6 %substitution.1 = (bf16[16,128,768]{2,1,0:T(8,128)(2,1)S(1)}, bf16[4,128,768]{2,1,0:T(8,128)(2,1)S(1)}) custom-call(s32[6,16]{1,0:T(8,128)} %bitcast.11, s32[4,8]{1,0:T(4,128)} %refs_1_.1, bf16[16,128,768]{2,1,0:T(8,128)(2,1)} %bitcast.8, bf16[4,128,768]{2,1,0:T(8,128)(2,1)} %bitcast.9, bf16[4,128,256]{2,1,0:T(8,128)(2,1)} %bitcast.10, ...), custom_call_target="tpu_custom_call" | custom-call | tf_op jit(solution)/shard_map/substitution/pallas_call | solution.py:451
  43.2 1.7 %copy.13 = bf16[2048,768]{1,0:T(8,128)(2,1)} copy(bf16[2048,768]{1,0:T(8,128)(2,1)S(1)} %bitcast.6) | data formatting | bytes 6291456
  44.9 0.9 %copy.14 = bf16[512,768]{1,0:T(8,128)(2,1)} copy(bf16[512,768]{1,0:T(8,128)(2,1)S(1)} %bitcast.7) | data formatting | bytes 1572864

commit v3 on v2

v3 whole, which is shorter than its diff:
```python
import jax
import jax.numpy as jnp
from jax import lax
from jax.experimental import pallas as pl
from jax.experimental.pallas import tpu as pltpu
from jax.sharding import PartitionSpec as P

BF = jnp.bfloat16
F32 = jnp.float32
MESH = pl.DeviceIdType.MESH
BL = 128
NI = 16
NL = 6
NJ = 4
NK = 8
NF = 16
NT = 3
CW = 256
HW = 128


def lanes(parts):
    return jnp.concatenate(parts, axis=1)


def rows(parts):
    return jnp.concatenate(parts, axis=0)


def mm(a, b):
    return jnp.dot(a, b, preferred_element_type=F32)


def source_of(slab, sub):
    return (sub + 2 * (slab % 8 == 0).astype(jnp.int32)) % 4


def shares_of(base):
    one = base + 1 - 2 * (base % 2)
    return (base, one, (base + 2) % 4, (one + 2) % 4)


def columns(t, c):
    return slice(t * CW + c * HW, t * CW + (c + 1) * HW)


def dense(cmat, front_half, shares):
    left = lanes([cmat[4 * sh + r] for sh in shares for r in range(4)])
    right = rows([front_half[pl.ds(4 * sh, 4)].reshape(4 * BL, HW) for sh in shares])
    return mm(left, right)


def interior(a, halves, iidx, i):
    left = lanes([a[i, k] for k in range(NL)])
    right = rows([lanes([half[iidx[k, i]] for half in halves]) for k in range(NL)])
    return mm(left, right)


def kernel(
    n_slab,
    iidx_h,
    oidx_h,
    rhs_h,
    front_h,
    pend_h,
    a_h,
    inv_h,
    b_h,
    finv_h,
    sol,
    fro,
    f20,
    f21,
    a,
    p2,
    cmat,
    w2,
    f00,
    f01,
    f10,
    f11,
    inv,
    b,
    finv,
    rhs,
    front,
    p32,
    pbf,
    w1,
    ysend,
    iidx,
    oidx,
    pos,
    load_sem,
    sent,
    recv_z,
    recv_x,
    recv_s,
    recv_xs,
):
    fr = ((f00, f01), (f10, f11), (f20, f21))
    w = (None, w1, w2)
    slab = lax.axis_index("slab")
    sub = lax.axis_index("sub")
    sib = sub + 1 - 2 * (sub % 2)
    xp = (sub + 2) % 4
    to_sub = (sub + 2 * ((slab + 1) % 8 == 0).astype(jnp.int32)) % 4
    from_sub = source_of(slab, sub)
    gives = slab < n_slab - 1
    takes = slab > 0
    sib_id = (slab, sib)
    x_id = (slab, xp)
    next_id = ((slab + 1) % n_slab, to_sub)
    prev_id = ((slab + n_slab - 1) % n_slab, from_sub)

    barrier = pltpu.get_barrier_semaphore()
    for peer in (sib_id, x_id):
        pl.semaphore_signal(barrier, inc=1, device_id=peer, device_id_type=MESH)

    @pl.when(takes)
    def _():
        pl.semaphore_signal(barrier, inc=1, device_id=prev_id, device_id_type=MESH)

    def share(t):
        return shares_of(sub if t == 0 else from_sub)

    loads = []

    def load(src, dst):
        copy = pltpu.make_async_copy(src, dst, load_sem.at[len(loads)])
        copy.start()
        loads.append(copy)
        return copy

    ld_idx = [load(iidx_h, iidx), load(oidx_h, oidx)]
    ld_inv = load(inv_h, inv)
    ld_a = [
        load(a_h.at[pl.ds(4 * g, 4)], a.at[pl.ds(4 * g, 4), pl.ds(0, NL)])
        for g in range(4)
    ]
    ld_finv = load(finv_h, finv)
    ld_b = load(b_h, b)
    ld_r = [load(rhs_h.at[:, :, 0:CW], rhs.at[0])]
    own = [
        load(
            pend_h.at[:, :, c * HW : (c + 1) * HW],
            fr[0][c].at[pl.ds(4 * sub, 4)],
        )
        for c in range(2)
    ]
    ld_g = load(front_h, front)

    def late_loads():
        for t in range(1, NT):
            ld_r.append(load(rhs_h.at[:, :, t * CW : (t + 1) * CW], rhs.at[t]))

    def send(src, dst, kind, got, peer):
        pltpu.make_async_remote_copy(
            src_ref=src,
            dst_ref=dst,
            send_sem=sent.at[kind],
            recv_sem=got,
            device_id=peer,
            device_id_type=MESH,
        ).start()

    def gated(when, body):
        if when is None:
            body()
        else:
            pl.when(when)(body)

    def taken(t):
        return takes if t else None

    def arrived(t, c, which, p, got):
        block = fr[t][c].at[4 * share(t)[which] + p]
        pltpu.make_async_copy(block, block, got).wait()

    def arrived_whole(t, c, which, got):
        def body():
            block = fr[t][c].at[pl.ds(4 * share(t)[which], 4)]
            pltpu.make_async_copy(block, block, got).wait()

        gated(taken(t), body)

    def greet():
        pl.semaphore_wait(barrier, 2 + gives.astype(jnp.int32))

    def gather(c):
        for p in range(NJ):
            src = pend_h.at[p, :, c * HW : (c + 1) * HW]
            dst = fr[0][c].at[4 * sub + p]
            send(src, dst, 0, recv_x.at[0, c, p], x_id)
        for p in range(NJ):
            src = pend_h.at[p, :, c * HW : (c + 1) * HW]
            dst = fr[0][c].at[4 * sub + p]
            send(src, dst, 0, recv_s.at[0, c], sib_id)

    def fwd_z(t, c, *ps):
        def body():
            for p in ps:
                got = recv_z.at[t - 1, c, p]
                arrived(t, c, 0, p, got)
                block = fr[t][c].at[4 * share(t)[0] + p]
                send(block, block, 1, recv_x.at[t, c, p], x_id)
                send(block, block, 1, recv_s.at[t, c], sib_id)

        gated(taken(t), body)

    def fwd_x(t, c, *ps):
        def body():
            for p in ps:
                arrived(t, c, 2, p, recv_x.at[t, c, p])
                block = fr[t][c].at[4 * share(t)[2] + p]
                send(block, block, min(t, 1), recv_xs.at[t, c], sib_id)

        gated(taken(t), body)

    def arr_s(t, c):
        arrived_whole(t, c, 1, recv_s.at[t, c])

    def arr_xs(t, c):
        arrived_whole(t, c, 3, recv_xs.at[t, c])

    def place(i, carry):
        own_links = [iidx[k, i] for k in range(NL)]
        for f in range(NF):
            at = jnp.int32(NL)
            for k in range(NL):
                at = jnp.where(own_links[k] == f, jnp.int32(k), at)
            pos[i * NF + f] = at
        return carry

    def places():
        for copy in ld_idx:
            copy.wait()
        lax.fori_loop(0, NI, place, 0)
        for i in range(NI):
            a[i, NL] = jnp.zeros((BL, BL), BF)

        @pl.when(slab == 0)
        def _():
            for t in range(1, NT):
                for c in range(2):
                    fr[t][c][...] = jnp.zeros((NF, BL, HW), BF)

    def a_wait(g):
        if g == 0:
            ld_inv.wait()
        ld_a[g].wait()

    def a_step(g):
        for i in range(4 * g, 4 * g + 4):
            for m in range(0, NL, 2):
                o = mm(inv[i], lanes([a[i, m], a[i, m + 1]]))
                o = (-o).astype(BF)
                a[i, m] = o[:, :BL]
                a[i, m + 1] = o[:, BL:]

    def b_wait():
        ld_finv.wait()
        ld_b.wait()

    def b_step():
        for j in range(NJ):
            for m in range(0, NK, 2):
                o = mm(finv[j], lanes([b[j, m], b[j, m + 1]]))
                o = (-o).astype(BF)
                b[j, m] = o[:, :BL]
                b[j, m + 1] = o[:, BL:]

    def c_step(*gs):
        for g in gs:
            for j in range(NJ):
                tiles = []
                for k in range(NK):
                    at = oidx[j, k]
                    tiles.append(
                        lanes(
                            [
                                a[at, pos[at * NF + 2 * g]],
                                a[at, pos[at * NF + 2 * g + 1]],
                            ]
                        )
                    )
                o = mm(lanes([b[j, k] for k in range(NK)]), rows(tiles)).astype(BF)
                cmat[2 * g, pl.ds(j * BL, BL)] = o[:, :BL]
                cmat[2 * g + 1, pl.ds(j * BL, BL)] = o[:, BL:]

    def p_step(t):
        ld_r[t].wait()
        for i in range(NI):
            o = mm(inv[i], rhs[t, i])
            if t < 2:
                p32[t, i] = o
            else:
                p2[i] = o
            if t:
                pbf[t - 1, i] = o.astype(BF)

    def front_left(j):
        return lanes([finv[j]] + [b[j, k] for k in range(NK)])

    def w_step(t):
        for j in range(NJ):
            right = rows(
                [front[j, :, t * CW : (t + 1) * CW]]
                + [pbf[t - 1, oidx[j, k]] for k in range(NK)]
            )
            o = mm(front_left(j), right)
            w[t][0, pl.ds(j * BL, BL)] = o[:, :HW]
            w[t][1, pl.ds(j * BL, BL)] = o[:, HW:]

    def acc2(t, c):
        arr_s(t, c)
        sh = share(t)
        w[t][c] = w[t][c] + dense(cmat, fr[t][c], sh[:2])

    def acc1(t, c):
        w[t][c] = w[t][c] + dense(cmat, fr[t][c], share(t)[2:3])

    def pass_on(t, c, *ps):
        def body():
            for p in ps:
                dst = fr[t + 1][c].at[4 * sub + p]
                got = recv_z.at[t, c, p]
                send(ysend.at[t, c, p], dst, 2, got, next_id)

        gated(gives, body)

    def y_step(t, c):
        arr_xs(t, c)
        sh = share(t)[3]
        right = fr[t][c][pl.ds(4 * sh, 4)].reshape(4 * BL, HW)
        for j in (0, 2):
            at = pl.ds(j * BL, 2 * BL)
            left = lanes([cmat[4 * sh + r, at] for r in range(4)])
            value = (w[t][c, at] + mm(left, right)).astype(BF).reshape(2, BL, HW)
            if t + 1 < NT:
                ysend[t, c, pl.ds(j, 2)] = value
                pass_on(t, c, j, j + 1)
            fro[j : j + 2, :, columns(t, c)] = value

    def s0_wait(c):
        own[c].wait()
        arr_s(0, c)
        arr_xs(0, c)

    def s0_step(c, *ids):
        for i in ids:
            base = p32[0, i, :, c * HW : (c + 1) * HW]
            o = base + interior(a, fr[0][c : c + 1], iidx, i)
            sol[i, :, columns(0, c)] = o.astype(BF)

    def y0_step(c):
        for j in range(NJ):
            right = rows(
                [front[j, :, columns(0, c)]]
                + [sol[oidx[j, k], :, columns(0, c)] for k in range(NK)]
            )
            value = mm(front_left(j), right).astype(BF)
            ysend[0, c, j] = value
            fro[j, :, columns(0, c)] = value
            if j % 2:
                pass_on(0, c, j - 1, j)

    def s_step(t, *ids):
        for i in ids:
            o = (p32[t, i] + interior(a, fr[t], iidx, i)).astype(BF)
            sol[i, :, t * CW : (t + 1) * CW] = o

    greet()
    gather(0)
    places()
    for g in range(4):
        a_wait(g)
        a_step(g)
    gather(1)
    late_loads()
    b_wait()
    b_step()
    p_step(0)
    fwd_x(0, 0, 0)
    c_step(0)
    fwd_x(0, 0, 1)
    c_step(1)
    fwd_x(0, 0, 2)
    ld_g.wait()
    fwd_x(0, 0, 3)
    c_step(2, 3)
    fwd_x(0, 1, 0)
    s0_wait(0)
    s0_step(0, *range(16))
    y0_step(0)
    fwd_x(0, 1, 1, 2, 3)
    c_step(4, 5)
    s0_wait(1)
    s0_step(1, *range(16))
    y0_step(1)
    fwd_z(1, 0, 0)
    c_step(6)
    fwd_z(1, 0, 1)
    c_step(7)
    fwd_z(1, 0, 2)
    p_step(1)
    fwd_z(1, 0, 3)
    w_step(1)
    fwd_z(1, 1, 0)
    acc2(1, 0)
    fwd_x(1, 0, 0)
    fwd_z(1, 1, 1)
    fwd_x(1, 0, 1)
    fwd_z(1, 1, 2)
    fwd_x(1, 0, 2)
    fwd_z(1, 1, 3)
    fwd_x(1, 0, 3)
    acc1(1, 0)
    fwd_x(1, 1, 0)
    y_step(1, 0)
    fwd_x(1, 1, 1)
    acc2(1, 1)
    fwd_x(1, 1, 2, 3)
    acc1(1, 1)
    y_step(1, 1)
    fwd_z(2, 0, 0)
    s_step(1, *range(0, 4))
    fwd_z(2, 0, 1)
    s_step(1, *range(4, 8))
    fwd_z(2, 0, 2)
    s_step(1, *range(8, 12))
    fwd_z(2, 0, 3)
    s_step(1, *range(12, 16))
    fwd_z(2, 1, 0)
    p_step(2)
    fwd_x(2, 0, 0)
    fwd_z(2, 1, 1)
    w_step(2)
    fwd_x(2, 0, 1)
    fwd_z(2, 1, 2)
    acc2(2, 0)
    fwd_x(2, 0, 2)
    fwd_z(2, 1, 3)
    fwd_x(2, 0, 3)
    acc1(2, 0)
    fwd_x(2, 1, 0)
    y_step(2, 0)
    fwd_x(2, 1, 1)
    acc2(2, 1)
    fwd_x(2, 1, 2, 3)
    acc1(2, 1)
    arr_xs(2, 1)

    def finish():
        def gone(kind, ref):
            pltpu.make_async_copy(ref, ref, sent.at[kind]).wait()

        gone(0, rhs.at[:, pl.ds(0, 4)])
        gated(takes, lambda: gone(1, rhs.at[:, pl.ds(0, 8)]))
        gated(gives, lambda: gone(2, ysend))

    finish()


def last(iidx_h, sol01, fro01, f20, f21, a, p2, cmat, w2, sol, fro, s, y, iidx, sem):
    moves = []

    def move(src, dst):
        copy = pltpu.make_async_copy(src, dst, sem.at[len(moves)])
        copy.start()
        moves.append(copy)
        return copy

    links = move(iidx_h, iidx)
    move(sol01, sol.at[:, :, : 2 * CW])
    cut = 2 * CW + HW
    move(fro01.at[:, :, :cut], fro.at[:, :, :cut])
    sh = shares_of(source_of(lax.axis_index("slab"), lax.axis_index("sub")))
    value = w2[1] + dense(cmat, f21, sh[3:])
    y[...] = value.astype(BF).reshape(NJ, BL, HW)
    move(y, fro.at[:, :, cut:])
    links.wait()
    for g in range(2):
        for i in range(8 * g, 8 * g + 8):
            s[i] = (p2[i] + interior(a, (f20, f21), iidx, i)).astype(BF)
        at = pl.ds(8 * g, 8)
        move(s.at[at], sol.at[at, :, 2 * CW :])
    for copy in moves[1:]:
        copy.wait()


def solution(mesh):
    n_slab = mesh.shape["slab"]

    def shards(rhs, front, pend, iidx, a, inv, oidx, b, finv):
        vmem = pl.BlockSpec(memory_space=pltpu.VMEM)
        hbm = pl.BlockSpec(memory_space=pltpu.HBM)
        dma = pltpu.SemaphoreType.DMA
        half = pltpu.VMEM((NF, BL, HW), BF)
        def in_hbm(x):
            return pltpu.with_memory_space_constraint(x, pltpu.HBM)

        def in_vmem(x):
            return pltpu.with_memory_space_constraint(x, pltpu.VMEM)

        iidx = in_hbm(iidx.T)
        made = pl.pallas_call(
            lambda *refs: kernel(n_slab, *refs),
            name="substitution",
            out_shape=(
                pltpu.VMEM((NI, BL, 2 * CW), BF),
                pltpu.VMEM((NJ, BL, NT * CW), BF),
                half,
                half,
                pltpu.VMEM((NI, NL + 1, BL, BL), BF),
                pltpu.VMEM((NI, BL, CW), F32),
                pltpu.VMEM((NF, NJ * BL, BL), BF),
                pltpu.VMEM((2, NJ * BL, HW), F32),
            ),
            in_specs=[hbm] * 9,
            out_specs=(vmem,) * 8,
            scratch_shapes=[half] * 4
            + [
                pltpu.VMEM((NI, BL, BL), BF),
                pltpu.VMEM((NJ, NK, BL, BL), BF),
                pltpu.VMEM((NJ, BL, BL), BF),
                pltpu.VMEM((NT, NI, BL, CW), BF),
                pltpu.VMEM((NJ, BL, NT * CW), BF),
                pltpu.VMEM((2, NI, BL, CW), F32),
                pltpu.VMEM((2, NI, BL, CW), BF),
                pltpu.VMEM((2, NJ * BL, HW), F32),
                pltpu.VMEM((2, 2, NJ, BL, HW), BF),
                pltpu.SMEM((NL, NI), jnp.int32),
                pltpu.SMEM((NJ, NK), jnp.int32),
                pltpu.SMEM((NI * NF,), jnp.int32),
                dma((15,)),
                dma((3,)),
                dma((NT - 1, 2, NJ)),
                dma((NT, 2, NJ)),
                dma((NT, 2)),
                dma((NT, 2)),
            ],
            compiler_params=pltpu.CompilerParams(
                collective_id=0,
                has_side_effects=True,
                vmem_limit_bytes=30 * 1024 * 1024,
            ),
        )(
            iidx,
            *(
                in_hbm(x)
                for x in (
                    oidx,
                    rhs.reshape(NI, BL, NT * CW),
                    front.reshape(NJ, BL, NT * CW),
                    pend.reshape(NJ, BL, CW),
                    a,
                    inv,
                    b,
                    finv,
                )
            )
        )
        sol, fro = pl.pallas_call(
            last,
            name="last",
            out_shape=(
                pltpu.HBM((NI, BL, NT * CW), BF),
                pltpu.HBM((NJ, BL, NT * CW), BF),
            ),
            in_specs=[hbm] + [vmem] * 8,
            out_specs=(hbm, hbm),
            scratch_shapes=[
                pltpu.VMEM((NI, BL, CW), BF),
                pltpu.VMEM((NJ, BL, HW), BF),
                pltpu.SMEM((NL, NI), jnp.int32),
                dma((6,)),
            ],
            compiler_params=pltpu.CompilerParams(
                vmem_limit_bytes=30 * 1024 * 1024,
            ),
        )(iidx, *(in_vmem(x) for x in made))
        return sol.reshape(NI * BL, NT * CW), fro.reshape(NJ * BL, NT * CW)

    both = ("slab", "sub")
    two = P(both, None)
    return jax.shard_map(
        shards,
        mesh=mesh,
        in_specs=(
            two,
            two,
            two,
            two,
            P(both, None, None, None),
            P(both, None, None),
            two,
            P(both, None, None, None),
            P(both, None, None),
        ),
        out_specs=(two, two),
        check_vma=False,
    )
```

time: 45.9 us -> 41.8 us (0.911)
  local copies, waits for them, and re-layouts: 2.55 us -> 0 us
  Pallas kernels: 42.6 us -> 40.9 us
    pallas_call x1, Pallas kernels: 42.6 us -> 37.9 us  [shards(): pl.pallas_call(lambda *refs: kernel(n_slab, *refs), name='substitution',...]
    pallas_call x0 -> x1, Pallas kernels: none -> 2.93 us  [shards(): pl.pallas_call(last, name='last', out_shape=(pltpu.HBM((NI, BL, NT * CW),...]
    unnamed x2 -> x0, local copies, waits for them, and re-layouts: 2.55 us -> none
where the time goes in v3:
time: 41.8 us; the launch traced here: 41.7 us
  Pallas kernels  40.9 us (98%)
  between operations  0.8 us (2%)
    pallas_call x1, Pallas kernels, shards(): pl.pallas_call(lambda *refs: kernel(n_slab, *refs), name='substitution',...  37.9 us
    pallas_call x1, Pallas kernels, shards(): pl.pallas_call(last, name='last', out_shape=(pltpu.HBM((NI, BL, NT * CW),...  2.93 us

profile of v3, /device:TPU:25, one launch (start us, length us, event | category | flops | bytes accessed | tf_op | source)
XLA Modules:
  0.0 41.7 jit_solution(5723421020224255455)
XLA Ops:
  0.6 37.9 %substitution.1 = (bf16[16,128,512]{2,1,0:T(8,128)(2,1)S(1)}, bf16[4,128,768]{2,1,0:T(8,128)(2,1)S(1)}, bf16[16,128,128]{2,1,0:T(8,128)(2,1)S(1)}, bf16[16,128,1...) custom-call(s32[6,16]{1,0:T(8,128)} %bitcast.9, ...), custom_call_target="tpu_custom_call" | custom-call | tf_op jit(solution)/shard_map/substitution/pallas_call | solution.py:507
  38.6 2.9 %last.1 = (bf16[16,128,768]{2,1,0:T(8,128)(2,1)}, bf16[4,128,768]{2,1,0:T(8,128)(2,1)}) custom-call(s32[6,16]{1,0:T(8,128)} %bitcast.10, bf16[16,128,512]{2,1,0:T(8,128)(2,1)S(1)} %get-tuple-element.12.sol01, bf16[4,128,768]{2,1,0:T(8,128)(2,1)S(1)} %get-tuple-element.13.fro01, bf16[16,128,128]{2,1,0:T(8,128)(2,1)S(1)} %get-tuple-element.14.f20, ...), custom_call_target="tpu_custom_call" | custom-call | tf_op jit(solution)/shard_map/last/pallas_call | solution.py:564

commit v4 on v3

--- a/solution.py
+++ b/solution.py
@@ -69,7 +69,6 @@
     finv_h,
     sol,
     fro,
-    f20,
     f21,
     a,
     p2,
@@ -79,6 +78,7 @@
     f01,
     f10,
     f11,
+    f20,
     inv,
     b,
     finv,
@@ -203,8 +203,8 @@
                 got = recv_z.at[t - 1, c, p]
                 arrived(t, c, 0, p, got)
                 block = fr[t][c].at[4 * share(t)[0] + p]
+                send(block, block, 1, recv_s.at[t, c], sib_id)
                 send(block, block, 1, recv_x.at[t, c, p], x_id)
-                send(block, block, 1, recv_s.at[t, c], sib_id)
 
         gated(taken(t), body)
 
@@ -339,7 +339,8 @@
             value = (w[t][c, at] + mm(left, right)).astype(BF).reshape(2, BL, HW)
             if t + 1 < NT:
                 ysend[t, c, pl.ds(j, 2)] = value
-                pass_on(t, c, j, j + 1)
+                if j:
+                    pass_on(t, c, *range(NJ))
             fro[j : j + 2, :, columns(t, c)] = value
 
     def s0_wait(c):
@@ -362,13 +363,17 @@
             value = mm(front_left(j), right).astype(BF)
             ysend[0, c, j] = value
             fro[j, :, columns(0, c)] = value
-            if j % 2:
-                pass_on(0, c, j - 1, j)
+        pass_on(0, c, *range(NJ))
 
     def s_step(t, *ids):
         for i in ids:
             o = (p32[t, i] + interior(a, fr[t], iidx, i)).astype(BF)
             sol[i, :, t * CW : (t + 1) * CW] = o
+
+    def s2_step():
+        for i in range(NI):
+            o = p2[i, :, :HW] + interior(a, fr[2][:1], iidx, i)
+            sol[i, :, columns(2, 0)] = o.astype(BF)
 
     greet()
     gather(0)
@@ -389,11 +394,10 @@
     ld_g.wait()
     fwd_x(0, 0, 3)
     c_step(2, 3)
-    fwd_x(0, 1, 0)
     s0_wait(0)
     s0_step(0, *range(16))
     y0_step(0)
-    fwd_x(0, 1, 1, 2, 3)
+    fwd_x(0, 1, 0, 1, 2, 3)
     c_step(4, 5)
     s0_wait(1)
     s0_step(1, *range(16))
@@ -411,14 +415,13 @@
     fwd_x(1, 0, 0)
     fwd_z(1, 1, 1)
     fwd_x(1, 0, 1)
+    fwd_x(1, 0, 2)
     fwd_z(1, 1, 2)
-    fwd_x(1, 0, 2)
+    fwd_x(1, 0, 3)
     fwd_z(1, 1, 3)
-    fwd_x(1, 0, 3)
     acc1(1, 0)
-    fwd_x(1, 1, 0)
     y_step(1, 0)
-    fwd_x(1, 1, 1)
+    fwd_x(1, 1, 0, 1)
     acc2(1, 1)
     fwd_x(1, 1, 2, 3)
     acc1(1, 1)
@@ -444,11 +447,12 @@
     fwd_x(2, 0, 3)
     acc1(2, 0)
     fwd_x(2, 1, 0)
+    acc2(2, 1)
+    fwd_x(2, 1, 1)
     y_step(2, 0)
-    fwd_x(2, 1, 1)
-    acc2(2, 1)
     fwd_x(2, 1, 2, 3)
     acc1(2, 1)
+    s2_step()
     arr_xs(2, 1)
 
     def finish():
@@ -462,7 +466,7 @@
     finish()
 
 
-def last(iidx_h, sol01, fro01, f20, f21, a, p2, cmat, w2, sol, fro, s, y, iidx, sem):
+def last(iidx_h, most, fro01, f21, a, p2, cmat, w2, sol, fro, s, y, iidx, sem):
     moves = []
 
     def move(src, dst):
@@ -471,20 +475,21 @@
         moves.append(copy)
         return copy
 
+    cut = NT * CW - HW
     links = move(iidx_h, iidx)
-    move(sol01, sol.at[:, :, : 2 * CW])
-    cut = 2 * CW + HW
+    move(most, sol.at[:, :, :cut])
     move(fro01.at[:, :, :cut], fro.at[:, :, :cut])
     sh = shares_of(source_of(lax.axis_index("slab"), lax.axis_index("sub")))
     value = w2[1] + dense(cmat, f21, sh[3:])
     y[...] = value.astype(BF).reshape(NJ, BL, HW)
     move(y, fro.at[:, :, cut:])
     links.wait()
-    for g in range(2):
-        for i in range(8 * g, 8 * g + 8):
-            s[i] = (p2[i] + interior(a, (f20, f21), iidx, i)).astype(BF)
-        at = pl.ds(8 * g, 8)
-        move(s.at[at], sol.at[at, :, 2 * CW :])
+    for first, count in ((0, 8), (8, 8)):
+        for i in range(first, first + count):
+            o = p2[i, :, HW:] + interior(a, (f21,), iidx, i)
+            s[i] = o.astype(BF)
+        at = pl.ds(first, count)
+        move(s.at[at], sol.at[at, :, cut:])
     for copy in moves[1:]:
         copy.wait()
 
@@ -508,9 +513,8 @@
             lambda *refs: kernel(n_slab, *refs),
             name="substitution",
             out_shape=(
-                pltpu.VMEM((NI, BL, 2 * CW), BF),
+                pltpu.VMEM((NI, BL, NT * CW - HW), BF),
                 pltpu.VMEM((NJ, BL, NT * CW), BF),
-                half,
                 half,
                 pltpu.VMEM((NI, NL + 1, BL, BL), BF),
                 pltpu.VMEM((NI, BL, CW), F32),
@@ -518,8 +522,8 @@
                 pltpu.VMEM((2, NJ * BL, HW), F32),
             ),
             in_specs=[hbm] * 9,
-            out_specs=(vmem,) * 8,
-            scratch_shapes=[half] * 4
+            out_specs=(vmem,) * 7,
+            scratch_shapes=[half] * 5
             + [
                 pltpu.VMEM((NI, BL, BL), BF),
                 pltpu.VMEM((NJ, NK, BL, BL), BF),
@@ -568,10 +572,10 @@
                 pltpu.HBM((NI, BL, NT * CW), BF),
                 pltpu.HBM((NJ, BL, NT * CW), BF),
             ),
-            in_specs=[hbm] + [vmem] * 8,
+            in_specs=[hbm] + [vmem] * 7,
             out_specs=(hbm, hbm),
             scratch_shapes=[
-                pltpu.VMEM((NI, BL, CW), BF),
+                pltpu.VMEM((NI, BL, HW), BF),
                 pltpu.VMEM((NJ, BL, HW), BF),
                 pltpu.SMEM((NL, NI), jnp.int32),
                 dma((6,)),

time: 41.8 us -> 41 us (0.981)
  Pallas kernels: 40.9 us -> 40 us
    pallas_call x1, Pallas kernels: 37.9 us -> 37.4 us  [shards(): pl.pallas_call(lambda *refs: kernel(n_slab, *refs), name='substitution',...]
where the time goes in v4:
time: 41 us; the launch traced here: 40.8 us
  Pallas kernels  40 us (98%)
  between operations  0.8 us (2%)
    pallas_call x1, Pallas kernels, shards(): pl.pallas_call(lambda *refs: kernel(n_slab, *refs), name='substitution',...  37.4 us
    pallas_call x1, Pallas kernels, shards(): pl.pallas_call(last, name='last', out_shape=(pltpu.HBM((NI, BL, NT * CW),...  2.66 us

profile of v4, /device:TPU:25, one launch (start us, length us, event | category | flops | bytes accessed | tf_op | source)
XLA Modules:
  0.0 40.8 jit_solution(13032824968636617917)
XLA Ops:
  0.6 37.4 %substitution.1 = (bf16[16,128,640]{2,1,0:T(8,128)(2,1)S(1)}, bf16[4,128,768]{2,1,0:T(8,128)(2,1)S(1)}, bf16[16,128,128]{2,1,0:T(8,128)(2,1)S(1)}, bf16[16,7,128...) custom-call(s32[6,16]{1,0:T(8,128)} %bitcast.9, ...), custom_call_target="tpu_custom_call" | custom-call | tf_op jit(solution)/shard_map/substitution/pallas_call | solution.py:512
  38.0 2.7 %last.1 = (bf16[16,128,768]{2,1,0:T(8,128)(2,1)}, bf16[4,128,768]{2,1,0:T(8,128)(2,1)}) custom-call(s32[6,16]{1,0:T(8,128)} %bitcast.10, bf16[16,128,640]{2,1,0:T(8,128)(2,1)S(1)} %get-tuple-element.11.most, bf16[4,128,768]{2,1,0:T(8,128)(2,1)S(1)} %get-tuple-element.12.fro01, bf16[16,128,128]{2,1,0:T(8,128)(2,1)S(1)} %get-tuple-element.13.f21, ...), custom_call_target="tpu_custom_call" | custom-call | tf_op jit(solution)/shard_map/last/pallas_call | solution.py:568

commit v5 on v4

--- a/solution.py
+++ b/solution.py
@@ -484,7 +484,7 @@
     y[...] = value.astype(BF).reshape(NJ, BL, HW)
     move(y, fro.at[:, :, cut:])
     links.wait()
-    for first, count in ((0, 8), (8, 8)):
+    for first, count in ((0, 12), (12, 4)):
         for i in range(first, first + count):
             o = p2[i, :, HW:] + interior(a, (f21,), iidx, i)
             s[i] = o.astype(BF)

time: 41 us -> 40.9 us (level)
  no operation moved by 1% of the time
where the time goes in v5:
time: 40.9 us; the launch traced here: 40.8 us
  Pallas kernels  40 us (98%)
  between operations  0.8 us (2%)
    pallas_call x1, Pallas kernels, shards(): pl.pallas_call(lambda *refs: kernel(n_slab, *refs), name='substitution',...  37.4 us
    pallas_call x1, Pallas kernels, shards(): pl.pallas_call(last, name='last', out_shape=(pltpu.HBM((NI, BL, NT * CW),...  2.62 us

profile of v5, /device:TPU:25, one launch (start us, length us, event | category | flops | bytes accessed | tf_op | source)
XLA Modules:
  0.0 40.8 jit_solution(536751974748729435)
XLA Ops:
  0.6 37.4 %substitution.1 = (bf16[16,128,640]{2,1,0:T(8,128)(2,1)S(1)}, bf16[4,128,768]{2,1,0:T(8,128)(2,1)S(1)}, bf16[16,128,128]{2,1,0:T(8,128)(2,1)S(1)}, bf16[16,7,128...) custom-call(s32[6,16]{1,0:T(8,128)} %bitcast.9, ...), custom_call_target="tpu_custom_call" | custom-call | tf_op jit(solution)/shard_map/substitution/pallas_call | solution.py:512
  38.0 2.6 %last.1 = (bf16[16,128,768]{2,1,0:T(8,128)(2,1)}, bf16[4,128,768]{2,1,0:T(8,128)(2,1)}) custom-call(s32[6,16]{1,0:T(8,128)} %bitcast.10, bf16[16,128,640]{2,1,0:T(8,128)(2,1)S(1)} %get-tuple-element.11.most, bf16[4,128,768]{2,1,0:T(8,128)(2,1)S(1)} %get-tuple-element.12.fro01, bf16[16,128,128]{2,1,0:T(8,128)(2,1)S(1)} %get-tuple-element.13.f21, ...), custom_call_target="tpu_custom_call" | custom-call | tf_op jit(solution)/shard_map/last/pallas_call | solution.py:568
